TPU v7x, 32 devices: a whole 2x2x4 slice. The times are simulated.
32 devices in a mesh: req: 4 (over z), row: 4 (over y, core), col: 2 (over x).
Axes of the slice: x: 2, y: 2, z: 4, core: 2. Of those that a mesh axis runs over, the one named last changes fastest.
Arguments:
- hidden: bfloat16 [1024, 2048], P(('req', 'row')), may hold values from -6 to 6
- latent_cache: bfloat16 [16, 384, 576], P('req'), may hold values from -144 to 144
- lengths: int32 [16], P('req'), may hold values from 96 to 384
- parents: int32 [16, 64], P('req'), may hold values from -1 to 62, as said below
- routes: int32 [1024, 6], P(('req', 'row')), may hold values from 0 to 15, all different within a row; in each aligned block of 64 rows (0 to 63, 64 to 127, ...) at most 48 rows name the same one
- accepted: int32 [16], P(('req', 'row')), may hold values from 0 to 63
- input_gain: float32 [2048], replicated, may hold values from 0.25 to 1.75
- query_weight: bfloat16 [2048, 3072], P(None, ('row', 'col')), may hold values from -0.125 to 0.125
- latent_weight: bfloat16 [2048, 576], replicated, may hold values from -0.125 to 0.125
- latent_gain: float32 [512], replicated, may hold values from 0.25 to 1.75
- key_absorb: bfloat16 [16, 128, 512], P(('row', 'col')), may hold values from -0.5 to 0.5
- value_absorb: bfloat16 [16, 512, 128], P(('row', 'col')), may hold values from -0.25 to 0.25
- output_weight: bfloat16 [2048, 2048], P(('row', 'col')), may hold values from -0.125 to 0.125
- post_gain: float32 [2048], replicated, may hold values from 0.25 to 1.75
- router_weight: bfloat16 [2048, 16], replicated, may hold values from -0.046875 to 0.046875
- shared_gate_up: bfloat16 [2, 2048, 2816], P(None, None, ('row', 'col')), may hold values from -0.125 to 0.125
- shared_down: bfloat16 [2816, 2048], P(('row', 'col')), may hold values from -0.109375 to 0.109375
- expert_gate_up: bfloat16 [16, 2, 2048, 1408], P(('req', 'row'), None, None, 'col'), may hold values from -0.125 to 0.125
- expert_down: bfloat16 [16, 1408, 2048], P(('req', 'row'), 'col'), may hold values from -1.5 to 1.5
Outputs:
- layer_output: bfloat16 [1024, 2048], P(('req', 'row'))
- accepted_latents: bfloat16 [16, 64, 576], P(('req', 'row'))
Inputs may be any that keep to these rules, and one draw needn't show every extreme that they name: parents[r, 0] is -1 and parents[r, i] lies in 0 to i - 1 for i >= 1. `routes`: the 6 experts of a token differ; within the 64 rows of one index of req and row no expert is named by more than 48 rows.
All inputs are finite; a program needn't handle non-finite values.
Results may differ from a plain program's by a relative error of at most 0.009.
The roundings to bfloat16 on the way count: a program that leaves them out, or rounds other values in their place, can miss the bound.
Values may be sent and summed in bfloat16 or wider, within the bound.
No kernel may reach another device: no remote copies, remote signals or barrier semaphores. Data moves between devices by JAX's collectives and lax.ppermute only.
A program may use at most 128 MiB of HBM per device.

v0:
```python
import math
import jax
import jax.numpy as jnp
from jax import lax
from jax.sharding import PartitionSpec as P

NOPE = 128
ROPE = 64
LAT = 512
VDIM = 128
CACHE = 384
WINDOW = 160
SINK = 4
EPSILON = 1e-06


def rms_scale(values, gain_row):
    mean_square = jnp.mean(values * values, axis=-1, keepdims=True)
    return values * lax.rsqrt(mean_square + EPSILON) * gain_row


def rope_tables(positions, rope_width):
    half_width = rope_width // 2
    frequency = jnp.exp(
        jnp.arange(half_width, dtype=jnp.float32) * (-2.0 * math.log(10000.0) / rope_width)
    )
    angles = positions[..., None] * frequency
    return (jnp.cos(angles), jnp.sin(angles))


def rotate(values, cosine, sine_part):
    half_width = values.shape[-1] // 2
    first_half = values[..., :half_width]
    second_half = values[..., half_width:]
    return jnp.concatenate(
        [
            first_half * cosine - second_half * sine_part,
            second_half * cosine + first_half * sine_part,
        ],
        axis=-1,
    )


def ancestry(parents):
    tree_size = parents.shape[-1]
    node_ids = jnp.arange(tree_size, dtype=jnp.int32)
    links = (parents[..., :, None] == node_ids[None, :]).astype(jnp.float32)
    closure = links + jnp.eye(tree_size, dtype=jnp.float32)
    for repeat in range(max(1, (tree_size - 1).bit_length())):
        closure = jnp.minimum(
            jnp.einsum("...ij,...jk->...ik", closure, closure, precision=lax.Precision.HIGHEST), 1.0
        )
    depths = jnp.sum(closure, axis=-1) - 1.0
    return (closure, depths)


def gather_rows(values):
    return lax.all_gather(values, "row", axis=0, tiled=True)


def project_down(values, weight):
    return lax.psum_scatter(
        jnp.dot(values, weight, preferred_element_type=jnp.float32),
        "row",
        scatter_dimension=0,
        tiled=True,
    )


def col_total(values):
    return lax.psum(values, "col")


def body(
    hidden,
    latent_cache,
    lengths,
    parents,
    routes,
    accepted,
    input_gain,
    query_weight,
    latent_weight,
    latent_gain,
    key_absorb,
    value_absorb,
    output_weight,
    post_gain,
    router_weight,
    shared_gate_up,
    shared_down,
    expert_gate_up,
    expert_down,
):
    tok_rows = hidden.shape[0]
    model_width = hidden.shape[1]
    group_reqs, tree_size = parents.shape
    head_count = key_absorb.shape[0]
    scale_factor = 1.0 / math.sqrt(NOPE + ROPE)
    normed = rms_scale(hidden.astype(jnp.float32), input_gain).astype(jnp.bfloat16)
    group_rows = gather_rows(normed)
    closure, depths = ancestry(parents)
    queries = jnp.dot(group_rows, query_weight, preferred_element_type=jnp.float32).astype(
        jnp.bfloat16
    )
    queries = queries.reshape(group_reqs, tree_size, head_count, NOPE + ROPE)
    projected = jnp.dot(group_rows, latent_weight, preferred_element_type=jnp.float32).reshape(
        group_reqs, tree_size, LAT + ROPE
    )
    positions = lengths.astype(jnp.float32)[:, None] + depths
    cosine, sine_part = rope_tables(positions, ROPE)
    content = rms_scale(projected[..., :LAT], latent_gain)
    key_rope = rotate(projected[..., LAT:], cosine, sine_part)
    fresh_latents = jnp.concatenate([content, key_rope], axis=-1).astype(jnp.bfloat16)
    query_latent = jnp.einsum(
        "rthn,hnl->rthl", queries[..., :NOPE], key_absorb, preferred_element_type=jnp.float32
    ).astype(jnp.bfloat16)
    query_rope = rotate(
        queries[..., NOPE:].astype(jnp.float32), cosine[:, :, None, :], sine_part[:, :, None, :]
    ).astype(jnp.bfloat16)
    query_full = jnp.concatenate([query_latent, query_rope], axis=-1)
    key_rows = jnp.concatenate([latent_cache, fresh_latents], axis=1)
    scores = (
        jnp.einsum("rthc,rkc->rhtk", query_full, key_rows, preferred_element_type=jnp.float32)
        * scale_factor
    )
    cache_spots = jnp.arange(CACHE, dtype=jnp.int32)[None, :]
    length_col = lengths[:, None]
    cache_allowed = (cache_spots < length_col) & (
        (cache_spots < SINK) | (cache_spots >= length_col - WINDOW)
    )
    allowed = jnp.concatenate(
        [
            jnp.broadcast_to(cache_allowed[:, None, :], (group_reqs, tree_size, CACHE)),
            closure > 0.5,
        ],
        axis=-1,
    )
    scores = jnp.where(allowed[:, None], scores, -1e30)
    row_peak = jnp.max(scores, axis=-1, keepdims=True)
    weights = jnp.exp(scores - row_peak)
    attention_weights = (weights / jnp.sum(weights, axis=-1, keepdims=True)).astype(jnp.bfloat16)
    out_latent = jnp.einsum(
        "rhtk,rkl->rthl", attention_weights, key_rows[..., :LAT], preferred_element_type=jnp.float32
    ).astype(jnp.bfloat16)
    head_output = jnp.einsum(
        "rthl,hlv->rthv", out_latent, value_absorb, preferred_element_type=jnp.float32
    ).astype(jnp.bfloat16)
    head_rows = head_output.reshape(group_reqs * tree_size, head_count * VDIM)
    attention_part = project_down(head_rows, output_weight)
    residual = hidden.astype(jnp.float32) + col_total(attention_part)
    post_normed = rms_scale(residual, post_gain).astype(jnp.bfloat16)
    router = jax.nn.softmax(
        jnp.dot(post_normed, router_weight, preferred_element_type=jnp.float32), axis=-1
    )
    experts = router_weight.shape[1]
    top_count = routes.shape[1]
    capacity = min(tok_rows, max(2, 2 * tok_rows * top_count // experts))
    labels = jnp.arange(experts, dtype=jnp.int32)
    chosen = jnp.sum((routes[:, :, None] == labels[None, None, :]).astype(jnp.float32), axis=1)
    row_order = jnp.arange(tok_rows, dtype=jnp.int32)
    earlier = (row_order[None, :] < row_order[:, None]).astype(jnp.float32)
    slot_rank = jnp.dot(earlier, chosen, precision=lax.Precision.HIGHEST)
    slot_ids = jnp.arange(capacity, dtype=jnp.float32)
    placing = (chosen.T[:, None, :] > 0.5) & (slot_rank.T[:, None, :] == slot_ids[None, :, None])
    outbound = jnp.einsum(
        "est,td->esd", placing.astype(jnp.bfloat16), post_normed, preferred_element_type=jnp.float32
    ).astype(jnp.bfloat16)
    inbound = lax.all_to_all(outbound, ("req", "row"), split_axis=0, concat_axis=0, tiled=True)
    group_post = gather_rows(post_normed)
    shared_gate = jnp.dot(group_post, shared_gate_up[0], preferred_element_type=jnp.float32)
    shared_upper = jnp.dot(group_post, shared_gate_up[1], preferred_element_type=jnp.float32)
    shared_hidden = (jax.nn.silu(shared_gate) * shared_upper).astype(jnp.bfloat16)
    shared_part = project_down(shared_hidden, shared_down)
    sources = inbound.shape[0]
    slot_rows = inbound.reshape(sources * capacity, model_width)
    expert_gate = jnp.dot(slot_rows, expert_gate_up[0, 0], preferred_element_type=jnp.float32)
    expert_upper = jnp.dot(slot_rows, expert_gate_up[0, 1], preferred_element_type=jnp.float32)
    expert_hidden = (jax.nn.silu(expert_gate) * expert_upper).astype(jnp.bfloat16)
    expert_result = jnp.dot(
        expert_hidden, expert_down[0], preferred_element_type=jnp.float32
    ).reshape(sources, capacity, model_width)
    returned = lax.all_to_all(
        expert_result.astype(jnp.bfloat16), ("req", "row"), split_axis=0, concat_axis=0, tiled=True
    ).astype(expert_result.dtype)
    weighting = placing.astype(jnp.float32) * router.T[:, None, :]
    routed = jnp.einsum("est,esd->td", weighting, returned, precision=lax.Precision.HIGHEST)
    summed_parts = col_total(shared_part + routed)
    layer_output = (residual + summed_parts).astype(jnp.bfloat16)
    own_count = accepted.shape[0]
    own_start = lax.axis_index("row") * own_count
    own_closure = lax.dynamic_slice_in_dim(closure, own_start, own_count, 0)
    own_depths = lax.dynamic_slice_in_dim(depths, own_start, own_count, 0)
    own_fresh = lax.dynamic_slice_in_dim(fresh_latents, own_start, own_count, 0)
    chooser = (jnp.arange(tree_size, dtype=jnp.int32)[None, :] == accepted[:, None]).astype(
        jnp.float32
    )
    path_mask = jnp.einsum("qi,qij->qj", chooser, own_closure, precision=lax.Precision.HIGHEST)
    levels = jnp.arange(tree_size, dtype=jnp.float32)
    path_places = path_mask[:, None, :] * (own_depths[:, None, :] == levels[None, :, None]).astype(
        jnp.float32
    )
    accepted_latents = jnp.einsum(
        "qkj,qjc->qkc",
        path_places.astype(jnp.bfloat16),
        own_fresh,
        preferred_element_type=jnp.float32,
    ).astype(jnp.bfloat16)
    return (layer_output, accepted_latents)


def solution(mesh):
    placed = (
        P(("req", "row"), None),
        P("req", None, None),
        P("req"),
        P("req", None),
        P(("req", "row"), None),
        P(("req", "row")),
        P(),
        P(None, ("row", "col")),
        P(),
        P(),
        P(("row", "col"), None, None),
        P(("row", "col"), None, None),
        P(("row", "col"), None),
        P(),
        P(),
        P(None, None, ("row", "col")),
        P(("row", "col"), None),
        P(("req", "row"), None, None, "col"),
        P(("req", "row"), "col", None),
    )
    return jax.shard_map(
        body,
        mesh=mesh,
        in_specs=placed,
        out_specs=(P(("req", "row"), None), P(("req", "row"), None, None)),
        check_vma=False,
    )
```

profile of v0, /device:TPU:0, one launch (start us, length us, event | category | flops | bytes accessed | tf_op | source)
XLA Modules:
  0.0 329.5 jit_solution(12373238078999165010)
XLA Ops:
  7.2 1.3 fusion.52
  8.5 1.8 fusion.54
  10.4 0.7 broadcast_add_fusion.2
  11.1 1.1 convolution_minimum_fusion.5
  12.2 0.3 convolution_minimum_fusion.4
  12.5 3.9 %copy.34 = bf16[4,384,576]{2,1,0:T(8,128)(2,1)} copy(bf16[4,384,576]{1,2,0:T(8,128)(2,1)} %param.20) | data formatting | bytes 3538944 | tf_op args[1]
  16.5 0.3 convolution_minimum_fusion.3
  16.8 0.3 convolution_minimum_fusion.2
  17.0 0.3 convolution_minimum_fusion.1
  17.3 0.4 fusion.110
  17.7 0.7 pad_add_fusion
  18.4 0.6 broadcast_add_fusion
  19.0 11.0 %all-gather.3.cloned.1.call-done = bf16[256,2048]{1,0:T(8,128)(2,1)} async-done(((bf16[64,2048]{1,0:T(8,128)(2,1)}), bf16[256,2048]{1,0:T(8,128)(2,1)}) %all-gather.3.cloned.1.call-update) | async-done | bytes 1048592 | tf_op jit(solution)/shard_map/all_gather | solution.py:58
  30.0 2.4 convolution_convert_fusion.3
  32.4 0.2 reshape.209
  32.7 3.0 fusion.117
  36.1 0.6 multiply_cosine_fusion
  36.7 0.8 slice-done
  37.5 1.1 fusion.32
  38.5 0.8 subtract_convert_fusion
  39.3 1.7 maximum_maximum_fusion
  41.0 3.8 %fusion.111 = (f32[4,2,64]{2,1,0:T(2,128)S(1)}, f32[4,2,64,448]{3,2,1,0:T(8,128)}) fusion(bf16[4,448,576]{2,1,0:T(8,128)(2,1)} %maximum_maximum_fusion, bf16[4,64,2,32]{3,1,2,0:T(8,128)(2,1)} %get-tuple-element.5, bf16[4,64,2,32]{3,1,2,0:T(8,128)(2,1)S(1)} %get-tuple-element.4, bf16[4,64,2,512]{3,1,2,0:T(8,128)(2,1)} %fusion.32, ...), kind=kOutput, calls=%fused_computation.152 | convolution fusion | flops 266928576 | bytes 3688448 | tf_op jit(solution)/shard_map/sub | solution.py:141
  44.8 2.5 fusion.45
  47.5 3.1 fusion.76
  50.6 31.5 %reduce-scatter.3.cloned.1.call-done = f32[64,2048]{1,0:T(8,128)} async-done(((f32[256,2048]{1,0:T(8,128)}), f32[64,2048]{1,0:T(8,128)}) %reduce-scatter.3.cloned.1.call-update) | async-done | bytes 524304 | tf_op jit(solution)/shard_map/reduce_scatter | solution.py:62
  82.3 30.8 %all-reduce.3.cloned.1.call-done = f32[64,2048]{1,0:T(8,128)} async-done(((f32[64,2048]{1,0:T(8,128)}), f32[64,2048]{1,0:T(8,128)}) %all-reduce.3.cloned.1.call-update) | async-done | bytes 524304 | tf_op jit(solution)/shard_map/psum | solution.py:71
  113.1 1.2 multiply_reduce_fusion
  114.3 1.2 multiply_convert_fusion.1
  115.5 2.7 convolution_convert_fusion.1
  118.2 5.7 %all-to-all-start = ((bf16[16,48,2048]{2,1,0:T(8,128)(2,1)}), bf16[16,48,2048]{2,1,0:T(8,128)(2,1)}, u32[]{:S(2)}, u32[]{:S(2)}) async-start(bf16[16,48,2048]{2,1,0:T(8,128)(2,1)} %convolution_convert_fusion.1), calls=%async_computation.2 | async-start | bytes 6291456 | tf_op jit(solution)/shard_map/all_to_all | solution.py:169
  123.9 0.2 all-gather.5.cloned.1.call-start
  124.1 0.3 all-gather.5.cloned.1.call-update
  124.5 58.9 %all-to-all-done = bf16[16,48,2048]{2,1,0:T(8,128)(2,1)} async-done(((bf16[16,48,2048]{2,1,0:T(8,128)(2,1)}), bf16[16,48,2048]{2,1,0:T(8,128)(2,1)}, u32[]{:S(2)}, u32[]{:S(2)}) %all-to-all-start) | async-done | bytes 3145760 | tf_op jit(solution)/shard_map/all_to_all | solution.py:169
  183.3 5.2 %fusion.4 = f32[768,704]{0,1:T(8,128)S(1)} fusion(bf16[768,2048]{1,0:T(8,128)(2,1)} %bitcast.16, bf16[1,2,2048,704]{2,3,1,0:T(8,128)(2,1)} %param.36), kind=kOutput, calls=%fused_computation.6 | convolution fusion | flops 2214592512 | bytes 8192000 | tf_op jit(solution)/shard_map/dot_general | solution.py:177
  188.6 6.3 %multiply_convert_fusion = bf16[768,704]{0,1:T(8,128)(2,1)} fusion(f32[768,704]{0,1:T(8,128)S(1)} %fusion.4, bf16[768,2048]{1,0:T(8,128)(2,1)} %bitcast.16, bf16[1,2,2048,704]{2,3,1,0:T(8,128)(2,1)} %param.36), kind=kOutput, calls=%fused_computation.15 | convolution fusion | flops 2217836544 | bytes 9273344 | tf_op jit(solution)/shard_map/dot_general | solution.py:178
  194.9 2.4 copy.39
  197.3 5.3 %convolution_convert_fusion = bf16[16,48,2048]{2,1,0:T(8,128)(2,1)} fusion(bf16[16,48,704]{2,1,0:T(8,128)(2,1)} %bitcast.141, bf16[1,704,2048]{2,1,0:T(8,128)(2,1)S(1)} %copy-done), kind=kOutput, calls=%fused_computation.1 | convolution fusion | flops 2216165376 | bytes 7110656 | tf_op jit(solution)/shard_map/dot_general | solution.py:180
  202.6 15.5 %all-to-all-start.1 = ((bf16[16,48,2048]{2,1,0:T(8,128)(2,1)}), bf16[16,48,2048]{2,1,0:T(8,128)(2,1)}, u32[]{:S(2)}, u32[]{:S(2)}) async-start(bf16[16,48,2048]{2,1,0:T(8,128)(2,1)} %convolution_convert_fusion), calls=%async_computation.3 | async-start | bytes 6291456 | tf_op jit(solution)/shard_map/all_to_all | solution.py:183
  218.2 3.0 fusion.17
  221.2 5.7 %fusion.43 = f32[256,2048]{1,0:T(8,128)} fusion(bf16[352,2048]{1,0:T(8,128)(2,1)} %param.35, bf16[256,2048]{1,0:T(8,128)(2,1)} %all-gather.5.cloned.1.call-done, bf16[2,2048,352]{1,2,0:T(8,128)(2,1)} %param.34, f32[256,352]{0,1:T(8,128)} %fusion.17), kind=kOutput, calls=%fused_computation.38 | convolution fusion | flops 738738176 | bytes 6389760 | tf_op jit(solution)/shard_map/dot_general | solution.py:63
  226.9 1.0 fusion.112
  228.0 38.3 %reduce-scatter.5.cloned.1.call-done = f32[64,2048]{1,0:T(8,128)} async-done(((f32[256,2048]{1,0:T(8,128)}), f32[64,2048]{1,0:T(8,128)}) %reduce-scatter.5.cloned.1.call-update) | async-done | bytes 524304 | tf_op jit(solution)/shard_map/reduce_scatter | solution.py:62
  266.3 11.3 %all-to-all-done.1 = bf16[16,48,2048]{2,1,0:T(8,128)(2,1)} async-done(((bf16[16,48,2048]{2,1,0:T(8,128)(2,1)}), bf16[16,48,2048]{2,1,0:T(8,128)(2,1)}, u32[]{:S(2)}, u32[]{:S(2)}) %all-to-all-start.1) | async-done | bytes 3145760 | tf_op jit(solution)/shard_map/all_to_all | solution.py:183
  277.6 4.6 %fusion.8 = f32[64,2048]{1,0:T(8,128)} fusion(f32[64,2048]{1,0:T(8,128)} %reduce-scatter.5.cloned.1.call-done, bf16[16,48,2048]{2,1,0:T(8,128)(2,1)} %all-to-all-done.1, f32[16,64]{1,0:T(8,128)S(1)} %divide_bitcast_fusion, f32[16,64]{1,0:T(8,128)S(1)} %fusion.91, pred[16,64]{1,0:T(8,128)(4,1)} %copy-done.12), kind=kOutput, calls=%fused_computation.11 | convolution fusion | flops 1208238080 | bytes 4203520 | tf_op jit(solution)/shard_map/est,esd->td/dot_general | solution.py:187
  283.0 0.7 fusion.102
  283.7 1.6 fusion.46
  285.3 35.4 %all-reduce.5.cloned.1.call-done = f32[64,2048]{1,0:T(8,128)} async-done(((f32[64,2048]{1,0:T(8,128)}), f32[64,2048]{1,0:T(8,128)}) %all-reduce.5.cloned.1.call-update) | async-done | bytes 524304 | tf_op jit(solution)/shard_map/psum | solution.py:71
  320.7 2.0 add_convert_fusion
  (64 shorter events, 1.4 us)
Async XLA Ops:
  7.2 190.1 %copy-start = (bf16[1,704,2048]{2,1,0:T(8,128)(2,1)S(1)}, bf16[1,704,2048]{2,1,0:T(8,128)(2,1)}, u32[]{:S(2)}) copy-start(bf16[1,704,2048]{2,1,0:T(8,128)(2,1)} %param.37) | copy-start | bytes 8650756
  7.2 22.8 %all-gather.3.cloned.1.call-start = ((), (), s32[]{:S(2)}) async-start(), calls=%async_computation.4 | async-start | bytes 1310720 | tf_op jit(solution)/shard_map/all_gather | solution.py:58
  10.3 6.1 %copy-start.15 = (s32[4]{0:T(128)S(1)}, s32[4]{0:T(128)}, u32[]{:S(2)}) copy-start(s32[4]{0:T(128)} %param.21) | copy-start | bytes 52
  10.3 71.8 %reduce-scatter.3.cloned.1.call-start = ((), (), s32[]{:S(2)}) async-start(), calls=%async_computation.5 | async-start | bytes 2621440 | tf_op jit(solution)/shard_map/reduce_scatter | solution.py:62
  32.6 3.1 copy-start.7
  32.7 3.2 copy-start.14
  35.7 1.0 copy-start.10
  35.8 3.6 %copy-start.1 = (bf16[4,384,576]{2,1,0:T(8,128)(2,1)S(1)}, bf16[4,384,576]{2,1,0:T(8,128)(2,1)}, u32[]{:S(2)}) copy-start(bf16[4,384,576]{2,1,0:T(8,128)(2,1)} %copy.34) | copy-start | bytes 5308420
  35.8 1.7 slice-start
  36.1 4.9 %copy-start.5 = (bf16[4,64,512]{2,1,0:T(8,128)(2,1)}, bf16[4,64,512]{2,1,0:T(8,128)(2,1)S(1)}, u32[]{:S(2)}) copy-start(bf16[4,64,512]{2,1,0:T(8,128)(2,1)S(1)} %multiply_convert_fusion.2) | copy-start | bytes 786436
  37.5 3.5 %copy-start.8 = (bf16[4,64,32]{2,1,0:T(8,128)(2,1)}, bf16[4,64,32]{2,1,0:T(8,128)(2,1)S(1)}, u32[]{:S(2)}) copy-start(bf16[4,64,32]{2,1,0:T(8,128)(2,1)S(1)} %get-tuple-element.8) | copy-start | bytes 49156
  37.5 3.5 %copy-start.9 = (bf16[4,64,32]{2,1,0:T(8,128)(2,1)}, bf16[4,64,32]{2,1,0:T(8,128)(2,1)S(1)}, u32[]{:S(2)}) copy-start(bf16[4,64,32]{2,1,0:T(8,128)(2,1)S(1)} %get-tuple-element.9) | copy-start | bytes 49156
  39.3 1.7 copy-start.11
  47.4 34.7 %copy-start.13 = (s32[64,6]{0,1:T(8,128)S(1)}, s32[64,6]{0,1:T(8,128)}, u32[]{:S(2)}) copy-start(s32[64,6]{0,1:T(8,128)} %param.23) | copy-start | bytes 4612
  47.4 65.7 %copy-start.2 = (bf16[64,2048]{1,0:T(8,128)(2,1)S(1)}, bf16[64,2048]{1,0:T(8,128)(2,1)}, u32[]{:S(2)}) copy-start(bf16[64,2048]{1,0:T(8,128)(2,1)} %param.19) | copy-start | bytes 786436
  50.5 62.6 %all-reduce.3.cloned.1.call-start = ((), (), s32[]{:S(2)}) async-start(), calls=%async_computation.6 | async-start | bytes 1048576 | tf_op jit(solution)/shard_map/psum | solution.py:71
  82.1 36.1 %copy-start.12 = (pred[16,64]{1,0:T(8,128)(4,1)}, pred[16,64]{1,0:T(8,128)(4,1)S(1)}, u32[]{:S(2)}) copy-start(pred[16,64]{1,0:T(8,128)(4,1)S(1)} %compare_bitcast_fusion) | copy-start | bytes 3076
  115.5 2.7 copy-start.3
  118.2 65.1 %all-to-all-start = ((bf16[16,48,2048]{2,1,0:T(8,128)(2,1)}), bf16[16,48,2048]{2,1,0:T(8,128)(2,1)}, u32[]{:S(2)}, u32[]{:S(2)}) async-start(bf16[16,48,2048]{2,1,0:T(8,128)(2,1)} %convolution_convert_fusion.1), calls=%async_computation.2 | async-start | bytes 6291456 | tf_op jit(solution)/shard_map/all_to_all | solution.py:169
  123.9 94.3 %all-gather.5.cloned.1.call-start = ((), (), s32[]{:S(2)}) async-start(), calls=%async_computation.7 | async-start | bytes 1310720 | tf_op jit(solution)/shard_map/all_gather | solution.py:58
  202.6 75.0 %all-to-all-start.1 = ((bf16[16,48,2048]{2,1,0:T(8,128)(2,1)}), bf16[16,48,2048]{2,1,0:T(8,128)(2,1)}, u32[]{:S(2)}, u32[]{:S(2)}) async-start(bf16[16,48,2048]{2,1,0:T(8,128)(2,1)} %convolution_convert_fusion), calls=%async_computation.3 | async-start | bytes 6291456 | tf_op jit(solution)/shard_map/all_to_all | solution.py:183
  218.1 48.3 %reduce-scatter.5.cloned.1.call-start = ((), (), s32[]{:S(2)}) async-start(), calls=%async_computation.8 | async-start | bytes 2621440 | tf_op jit(solution)/shard_map/reduce_scatter | solution.py:62
  221.2 5.7 %copy-start.4 = (bf16[64,2048]{1,0:T(8,128)(2,1)S(1)}, bf16[64,2048]{1,0:T(8,128)(2,1)}, u32[]{:S(2)}) copy-start(bf16[64,2048]{1,0:T(8,128)(2,1)} %copy-done.3) | copy-start | bytes 786436
  226.9 93.9 %all-reduce.5.cloned.1.call-start = ((), (), s32[]{:S(2)}) async-start(), calls=%async_computation.9 | async-start | bytes 1048576 | tf_op jit(solution)/shard_map/psum | solution.py:71
  228.0 55.7 %copy-start.6 = (bf16[4,64,512]{2,1,0:T(8,128)(2,1)S(1)}, bf16[4,64,512]{2,1,0:T(8,128)(2,1)}, u32[]{:S(2)}) copy-start(bf16[4,64,512]{2,1,0:T(8,128)(2,1)} %copy-done.5) | copy-start | bytes 786436
Sparse Core Ops, SparseCore 0:
  10.4 19.5 all-gather.2
  50.7 31.3 reduce-scatter.2
  84.5 28.5 all-reduce.2
  126.5 30.3 all-gather.4
  227.0 39.3 reduce-scatter.4
  282.4 38.2 all-reduce.4
where the time goes:
time: 330 us
  waiting for transfers between devices  218 us (66%)
  matrix products  54 us (16%)
  starting transfers between devices  21.6 us (7%)
  between operations  15.1 us (5%)
  other arithmetic  12.9 us (4%)
  local copies, waits for them, and re-layouts  8.26 us (3%)
    reduce_scatter x2, waiting for transfers between devices, project_down(): lax.psum_scatter(jnp.dot(values, weight, preferred_element_type=jnp.float...  69.8 us
    psum x2, waiting for transfers between devices, col_total(): return lax.psum(values, 'col')  66.2 us
    all_to_all x1, waiting for transfers between devices, body(): lax.all_to_all(outbound, ('req', 'row'), split_axis=0, concat_axis=0, til...  58.9 us
    all_to_all x1, starting transfers between devices, body(): lax.all_to_all(expert_result.astype(jnp.bfloat16), ('req', 'row'), split_...  15.5 us
    all_to_all x1, waiting for transfers between devices, body(): lax.all_to_all(expert_result.astype(jnp.bfloat16), ('req', 'row'), split_...  11.3 us
    all_gather x2, waiting for transfers between devices, gather_rows(): return lax.all_gather(values, 'row', axis=0, tiled=True)  11 us
    dot_general x2, matrix products, project_down(): jnp.dot(values, weight, preferred_element_type=jnp.float32)  8.71 us
  transfers between devices with their start and end apart: 8, of which 7 were waited for; matrix products, arithmetic and copies ran while one was open for 12% of the time, Pallas kernels for 0%

commit v1 on v0

--- a/solution.py
+++ b/solution.py
@@ -12,6 +12,12 @@
 WINDOW = 160
 SINK = 4
 EPSILON = 1e-06
+
+
+def summed_here(array, mesh_axis):
+    parts = lax.all_gather(array, mesh_axis, axis=0, tiled=False)
+    result = parts.sum(axis=0)
+    return result
 
 
 def rms_scale(values, gain_row):
@@ -68,7 +74,7 @@
 
 
 def col_total(values):
-    return lax.psum(values, "col")
+    return summed_here(values, "col")
 
 
 def body(

time: 330 us -> 319 us (0.967)
  waiting for transfers between devices: 218 us -> 202 us
  other arithmetic: 12.9 us -> 16.9 us
    psum x2 -> x0, waiting for transfers between devices: 66.2 us -> none  [col_total(): return lax.psum(values, 'col')]
    all_gather x0 -> x2, waiting for transfers between devices: none -> 50.8 us  [summed_here(): parts = lax.all_gather(array, mesh_axis, axis=0, tiled=False)]
    reduce_sum x0 -> x2, other arithmetic: none -> 3.49 us  [summed_here(): result = parts.sum(axis=0)]
  transfers between devices with their start and end apart: 8 -> 8, of which waited for: 7 -> 7; matrix products, arithmetic and copies ran while one was open for 12% -> 13% of each run, Pallas kernels for 0% -> 0%
where the time goes in v1:
time: 319 us; the launch traced here: 318 us
  waiting for transfers between devices  202 us (63%)
  matrix products  54.1 us (17%)
  starting transfers between devices  21.6 us (7%)
  other arithmetic  16.9 us (5%)
  between operations  15.1 us (5%)
  local copies, waits for them, and re-layouts  8.24 us (3%)
    reduce_scatter x2, waiting for transfers between devices, project_down(): lax.psum_scatter(jnp.dot(values, weight, preferred_element_type=jnp.float...  69.8 us
    all_to_all x1, waiting for transfers between devices, body(): lax.all_to_all(outbound, ('req', 'row'), split_axis=0, concat_axis=0, til...  58.9 us
    all_gather x2, waiting for transfers between devices, summed_here(): parts = lax.all_gather(array, mesh_axis, axis=0, tiled=False)  50.8 us
    all_to_all x1, starting transfers between devices, body(): lax.all_to_all(expert_result.astype(jnp.bfloat16), ('req', 'row'), split_...  15.5 us
    all_to_all x1, waiting for transfers between devices, body(): lax.all_to_all(expert_result.astype(jnp.bfloat16), ('req', 'row'), split_...  11.3 us
    all_gather x2, waiting for transfers between devices, gather_rows(): return lax.all_gather(values, 'row', axis=0, tiled=True)  11 us
    dot_general x2, matrix products, project_down(): jnp.dot(values, weight, preferred_element_type=jnp.float32)  8.6 us
  transfers between devices with their start and end apart: 8, of which 7 were waited for; matrix products, arithmetic and copies ran while one was open for 13% of the time, Pallas kernels for 0%

profile of v1, /device:TPU:0, one launch (start us, length us, event | category | flops | bytes accessed | tf_op | source)
XLA Modules:
  0.0 318.1 jit_solution(13013918573702020785)
XLA Ops:
  7.2 1.3 fusion.52
  8.5 1.8 fusion.54
  10.4 0.7 broadcast_add_fusion.2
  11.1 1.1 convolution_minimum_fusion.5
  12.3 0.3 convolution_minimum_fusion.4
  12.5 3.9 %copy.34 = bf16[4,384,576]{2,1,0:T(8,128)(2,1)} copy(bf16[4,384,576]{1,2,0:T(8,128)(2,1)} %param.20) | data formatting | bytes 3538944 | tf_op args[1]
  16.5 0.3 convolution_minimum_fusion.3
  16.8 0.3 convolution_minimum_fusion.2
  17.0 0.3 convolution_minimum_fusion.1
  17.3 0.4 fusion.110
  17.7 0.7 pad_add_fusion
  18.4 0.6 broadcast_add_fusion
  19.0 11.0 %all-gather.7.cloned.1.call-done = bf16[256,2048]{1,0:T(8,128)(2,1)} async-done(((bf16[64,2048]{1,0:T(8,128)(2,1)}), bf16[256,2048]{1,0:T(8,128)(2,1)}) %all-gather.7.cloned.1.call-update) | async-done | bytes 1048592 | tf_op jit(solution)/shard_map/all_gather | solution.py:64
  30.0 2.4 convolution_convert_fusion.3
  32.7 3.0 fusion.117
  36.1 0.6 multiply_cosine_fusion
  36.7 0.8 slice-done
  37.5 0.3 fusion.32
  37.8 0.8 subtract_convert_fusion
  38.6 1.7 maximum_maximum_fusion
  40.3 3.7 %fusion.111 = (f32[4,2,64]{2,1,0:T(2,128)S(1)}, f32[4,2,64,448]{3,2,1,0:T(8,128)}) fusion(bf16[4,448,576]{2,1,0:T(8,128)(2,1)} %maximum_maximum_fusion, bf16[4,64,2,32]{3,1,2,0:T(8,128)(2,1)} %get-tuple-element.5, bf16[4,64,2,32]{3,1,2,0:T(8,128)(2,1)} %get-tuple-element.4, bf16[4,64,2,512]{3,1,2,0:T(8,128)(2,1)S(1)} %fusion.32, ...), kind=kOutput, calls=%fused_computation.152 | convolution fusion | flops 266928576 | bytes 3688448 | tf_op jit(solution)/shard_map/sub | solution.py:147
  43.9 2.5 fusion.45
  46.6 3.0 fusion.76
  49.7 31.5 %reduce-scatter.3.cloned.1.call-done = f32[64,2048]{1,0:T(8,128)} async-done(((f32[256,2048]{1,0:T(8,128)}), f32[64,2048]{1,0:T(8,128)}) %reduce-scatter.3.cloned.1.call-update) | async-done | bytes 524304 | tf_op jit(solution)/shard_map/reduce_scatter | solution.py:68
  81.4 22.8 %all-gather.11.cloned.1.call-done = f32[128,2048]{1,0:T(8,128)} async-done(((f32[64,2048]{1,0:T(8,128)}), f32[128,2048]{1,0:T(8,128)}) %all-gather.11.cloned.1.call-update) | async-done | bytes 1048592 | tf_op jit(solution)/shard_map/all_gather | solution.py:18
  104.2 1.3 reduce_sum.85
  105.5 1.1 multiply_reduce_fusion
  106.6 1.8 multiply_convert_fusion.1
  108.4 3.6 %convolution_convert_fusion.1 = bf16[16,48,2048]{2,1,0:T(8,128)(2,1)} fusion(bf16[64,2048]{1,0:T(8,128)(2,1)} %multiply_convert_fusion.1, f32[16,64]{1,0:T(8,128)S(1)} %fusion.91, pred[16,64]{1,0:T(8,128)(4,1)S(1)} %compare_bitcast_fusion), kind=kOutput, calls=%fused_computation.2 | convolution fusion | flops 202997760 | bytes 3412992 | tf_op jit(solution)/shard_map/est,td->esd/dot_general | solution.py:172
  112.0 5.7 %all-to-all-start = ((bf16[16,48,2048]{2,1,0:T(8,128)(2,1)}), bf16[16,48,2048]{2,1,0:T(8,128)(2,1)}, u32[]{:S(2)}, u32[]{:S(2)}) async-start(bf16[16,48,2048]{2,1,0:T(8,128)(2,1)} %convolution_convert_fusion.1), calls=%async_computation.2 | async-start | bytes 6291456 | tf_op jit(solution)/shard_map/all_to_all | solution.py:175
  117.9 0.3 all-gather.9.cloned.1.call-update
  118.3 58.9 %all-to-all-done = bf16[16,48,2048]{2,1,0:T(8,128)(2,1)} async-done(((bf16[16,48,2048]{2,1,0:T(8,128)(2,1)}), bf16[16,48,2048]{2,1,0:T(8,128)(2,1)}, u32[]{:S(2)}, u32[]{:S(2)}) %all-to-all-start) | async-done | bytes 3145760 | tf_op jit(solution)/shard_map/all_to_all | solution.py:175
  177.2 5.2 %fusion.4 = f32[768,704]{0,1:T(8,128)S(1)} fusion(bf16[768,2048]{1,0:T(8,128)(2,1)} %bitcast.17, bf16[1,2,2048,704]{2,3,1,0:T(8,128)(2,1)} %param.36), kind=kOutput, calls=%fused_computation.6 | convolution fusion | flops 2214592512 | bytes 8192000 | tf_op jit(solution)/shard_map/dot_general | solution.py:183
  182.4 6.3 %multiply_convert_fusion = bf16[768,704]{0,1:T(8,128)(2,1)} fusion(f32[768,704]{0,1:T(8,128)S(1)} %fusion.4, bf16[768,2048]{1,0:T(8,128)(2,1)} %bitcast.17, bf16[1,2,2048,704]{2,3,1,0:T(8,128)(2,1)} %param.36), kind=kOutput, calls=%fused_computation.15 | convolution fusion | flops 2217836544 | bytes 9273344 | tf_op jit(solution)/shard_map/dot_general | solution.py:184
  188.7 2.4 copy.39
  191.1 5.3 %convolution_convert_fusion = bf16[16,48,2048]{2,1,0:T(8,128)(2,1)} fusion(bf16[16,48,704]{2,1,0:T(8,128)(2,1)} %bitcast.143, bf16[1,704,2048]{2,1,0:T(8,128)(2,1)S(1)} %copy-done), kind=kOutput, calls=%fused_computation.1 | convolution fusion | flops 2216165376 | bytes 7110656 | tf_op jit(solution)/shard_map/dot_general | solution.py:186
  196.3 15.5 %all-to-all-start.1 = ((bf16[16,48,2048]{2,1,0:T(8,128)(2,1)}), bf16[16,48,2048]{2,1,0:T(8,128)(2,1)}, u32[]{:S(2)}, u32[]{:S(2)}) async-start(bf16[16,48,2048]{2,1,0:T(8,128)(2,1)} %convolution_convert_fusion), calls=%async_computation.3 | async-start | bytes 6291456 | tf_op jit(solution)/shard_map/all_to_all | solution.py:189
  211.9 3.0 fusion.17
  214.9 5.6 %fusion.43 = f32[256,2048]{1,0:T(8,128)} fusion(bf16[352,2048]{1,0:T(8,128)(2,1)} %param.35, bf16[256,2048]{1,0:T(8,128)(2,1)} %all-gather.9.cloned.1.call-done, bf16[2,2048,352]{1,2,0:T(8,128)(2,1)} %param.34, f32[256,352]{0,1:T(8,128)} %fusion.17), kind=kOutput, calls=%fused_computation.38 | convolution fusion | flops 738738176 | bytes 6389760 | tf_op jit(solution)/shard_map/dot_general | solution.py:69
  220.6 1.1 fusion.112
  221.8 38.3 %reduce-scatter.5.cloned.1.call-done = f32[64,2048]{1,0:T(8,128)} async-done(((f32[256,2048]{1,0:T(8,128)}), f32[64,2048]{1,0:T(8,128)}) %reduce-scatter.5.cloned.1.call-update) | async-done | bytes 524304 | tf_op jit(solution)/shard_map/reduce_scatter | solution.py:68
  260.1 11.3 %all-to-all-done.1 = bf16[16,48,2048]{2,1,0:T(8,128)(2,1)} async-done(((bf16[16,48,2048]{2,1,0:T(8,128)(2,1)}), bf16[16,48,2048]{2,1,0:T(8,128)(2,1)}, u32[]{:S(2)}, u32[]{:S(2)}) %all-to-all-start.1) | async-done | bytes 3145760 | tf_op jit(solution)/shard_map/all_to_all | solution.py:189
  271.4 4.6 %fusion.8 = f32[64,2048]{1,0:T(8,128)} fusion(f32[64,2048]{1,0:T(8,128)} %reduce-scatter.5.cloned.1.call-done, bf16[16,48,2048]{2,1,0:T(8,128)(2,1)} %all-to-all-done.1, f32[16,64]{1,0:T(8,128)S(1)} %divide_bitcast_fusion, f32[16,64]{1,0:T(8,128)S(1)} %fusion.91, pred[16,64]{1,0:T(8,128)(4,1)} %copy-done.7), kind=kOutput, calls=%fused_computation.11 | convolution fusion | flops 1208238080 | bytes 4203520 | tf_op jit(solution)/shard_map/est,esd->td/dot_general | solution.py:193
  276.8 0.7 fusion.102
  277.5 1.7 fusion.46
  279.2 28.0 %all-gather.13.cloned.1.call-done = f32[128,2048]{1,0:T(8,128)} async-done(((f32[64,2048]{1,0:T(8,128)}), f32[128,2048]{1,0:T(8,128)}) %all-gather.13.cloned.1.call-update) | async-done | bytes 1048592 | tf_op jit(solution)/shard_map/all_gather | solution.py:18
  307.2 2.1 reduce_sum.89
  309.3 1.9 add_convert_fusion
  (56 shorter events, 1.7 us)
Async XLA Ops:
  7.2 183.9 %copy-start = (bf16[1,704,2048]{2,1,0:T(8,128)(2,1)S(1)}, bf16[1,704,2048]{2,1,0:T(8,128)(2,1)}, u32[]{:S(2)}) copy-start(bf16[1,704,2048]{2,1,0:T(8,128)(2,1)} %param.37) | copy-start | bytes 8650756
  7.2 22.8 %all-gather.7.cloned.1.call-start = ((), (), s32[]{:S(2)}) async-start(), calls=%async_computation.4 | async-start | bytes 1310720 | tf_op jit(solution)/shard_map/all_gather | solution.py:64
  10.3 6.1 %copy-start.10 = (s32[4]{0:T(128)S(1)}, s32[4]{0:T(128)}, u32[]{:S(2)}) copy-start(s32[4]{0:T(128)} %param.21) | copy-start | bytes 52
  10.3 70.9 %reduce-scatter.3.cloned.1.call-start = ((), (), s32[]{:S(2)}) async-start(), calls=%async_computation.5 | async-start | bytes 2621440 | tf_op jit(solution)/shard_map/reduce_scatter | solution.py:68
  32.6 3.1 copy-start.3
  32.7 3.2 %copy-start.9 = (f32[512]{0:T(512)S(1)}, f32[512]{0:T(512)}, u32[]{:S(2)}) copy-start(f32[512]{0:T(512)} %param.28) | copy-start | bytes 6148
  35.8 1.0 copy-start.6
  35.8 2.8 copy-start.1
  35.8 1.7 slice-start
  36.1 4.2 %copy-start.2 = (bf16[4,64,512]{2,1,0:T(8,128)(2,1)}, bf16[4,64,512]{2,1,0:T(8,128)(2,1)S(1)}, u32[]{:S(2)}) copy-start(bf16[4,64,512]{2,1,0:T(8,128)(2,1)S(1)} %multiply_convert_fusion.2) | copy-start | bytes 786436
  37.5 2.8 copy-start.4
  37.5 2.8 copy-start.5
  46.6 34.6 %copy-start.8 = (s32[64,6]{0,1:T(8,128)S(1)}, s32[64,6]{0,1:T(8,128)}, u32[]{:S(2)}) copy-start(s32[64,6]{0,1:T(8,128)} %param.23) | copy-start | bytes 4612
  49.6 54.5 %all-gather.11.cloned.1.call-start = ((), (), s32[]{:S(2)}) async-start(), calls=%async_computation.8 | async-start | bytes 1572864 | tf_op jit(solution)/shard_map/all_gather | solution.py:18
  81.3 30.8 %copy-start.7 = (pred[16,64]{1,0:T(8,128)(4,1)}, pred[16,64]{1,0:T(8,128)(4,1)S(1)}, u32[]{:S(2)}) copy-start(pred[16,64]{1,0:T(8,128)(4,1)S(1)} %compare_bitcast_fusion) | copy-start | bytes 3076
  112.0 65.1 %all-to-all-start = ((bf16[16,48,2048]{2,1,0:T(8,128)(2,1)}), bf16[16,48,2048]{2,1,0:T(8,128)(2,1)}, u32[]{:S(2)}, u32[]{:S(2)}) async-start(bf16[16,48,2048]{2,1,0:T(8,128)(2,1)} %convolution_convert_fusion.1), calls=%async_computation.2 | async-start | bytes 6291456 | tf_op jit(solution)/shard_map/all_to_all | solution.py:175
  117.7 94.2 %all-gather.9.cloned.1.call-start = ((), (), s32[]{:S(2)}) async-start(), calls=%async_computation.6 | async-start | bytes 1310720 | tf_op jit(solution)/shard_map/all_gather | solution.py:64
  196.3 75.0 %all-to-all-start.1 = ((bf16[16,48,2048]{2,1,0:T(8,128)(2,1)}), bf16[16,48,2048]{2,1,0:T(8,128)(2,1)}, u32[]{:S(2)}, u32[]{:S(2)}) async-start(bf16[16,48,2048]{2,1,0:T(8,128)(2,1)} %convolution_convert_fusion), calls=%async_computation.3 | async-start | bytes 6291456 | tf_op jit(solution)/shard_map/all_to_all | solution.py:189
  211.8 48.3 %reduce-scatter.5.cloned.1.call-start = ((), (), s32[]{:S(2)}) async-start(), calls=%async_computation.7 | async-start | bytes 2621440 | tf_op jit(solution)/shard_map/reduce_scatter | solution.py:68
  220.5 86.7 %all-gather.13.cloned.1.call-start = ((), (), s32[]{:S(2)}) async-start(), calls=%async_computation.9 | async-start | bytes 1572864 | tf_op jit(solution)/shard_map/all_gather | solution.py:18
Sparse Core Ops, SparseCore 0:
  10.4 19.5 all-gather.6
  49.8 31.3 reduce-scatter.2
  82.8 21.2 all-gather.10
  120.4 30.2 all-gather.8
  220.7 39.3 reduce-scatter.4
  276.1 31.0 all-gather.12
